TPU v7x, 128 devices: a whole 4x4x4 slice. The times are simulated.
128 devices in a mesh: shift: 4 (over z), leaf: 32 (over x, y, core).
Axes of the slice: x: 4, y: 4, z: 4, core: 2. Of those that a mesh axis runs over, the one named last changes fastest.
Arguments:
- leaf_rhs: bfloat16 [32, 1024, 1024], P('leaf'), may hold values from -6 to 6
- leaf_inverse: bfloat16 [4, 32, 1024, 1024], P('shift', 'leaf')
- leaf_coupling: bfloat16 [4, 32, 1024, 384], P('shift', 'leaf'), may hold values from -0.1875 to 0.1875
- leaf_rows: int32 [32, 384], P('leaf'), may hold values from 0 to 767, as said below
- front_sizes: int32 [5], replicated, may hold values from 384 to 768, as said below
- front_inverse: bfloat16 [4, 5, 32, 768, 768], P('shift', None, 'leaf'), as said below
- front_coupling: bfloat16 [4, 4, 32, 768, 768], P('shift', None, 'leaf'), as said below
- shift_weight: float32 [4], P('shift'), may hold values from -1 to 1
Outputs:
- filtered: float32 [32, 1024, 1024], P('leaf', 'shift')
Inputs may be any that keep to these rules, and one draw needn't show every extreme that they name: `leaf_rows`: the 384 entries of one leaf are distinct. `front_sizes`: the front of at least one level is full. `front_inverse`: all leaves below one separator hold the same front inverse for it. `front_coupling`: all leaves below one separator hold the same coupling for it.
All inputs are finite; a program needn't handle non-finite values.
Results may differ from a plain program's by a relative error of at most 0.01.
Values may be sent and summed in bfloat16 or wider, within the bound.
A program may use at most 128 MiB of HBM per device.

v0:
```python
import jax
import jax.numpy as jnp
from jax import lax
from jax.sharding import PartitionSpec as P


def partner_2(value, axis, stride):
    mask = 2**stride
    pairs = [(source, source ^ mask) for source in range(lax.axis_size(axis))]
    return lax.ppermute(value, axis, pairs)


def transposed(left_matrix, right_matrix):
    return lax.dot_general(
        left_matrix, right_matrix, (((0,), (0,)), ((), ())), preferred_element_type=jnp.float32
    )


def widen(solved, bit_index, position):
    partner = partner_2(solved, "leaf", bit_index)
    own_bit = position >> bit_index & 1
    lower = jnp.where(own_bit == 0, solved, partner)
    upper = jnp.where(own_bit == 0, partner, solved)
    return jnp.concatenate([lower, upper], axis=1)


def body(
    leaf_rhs,
    leaf_inverse,
    leaf_coupling,
    leaf_rows,
    front_sizes,
    front_inverse,
    front_coupling,
    shift_weight,
):
    levels = lax.axis_size("leaf").bit_length() - 1
    position = lax.axis_index("leaf")
    inverse = leaf_inverse[0, 0]
    coupling = leaf_coupling[0, 0]
    front = front_inverse.shape[-1]
    selector = (leaf_rows[0][:, None] == jnp.arange(front, dtype=jnp.int32)[None, :]).astype(
        jnp.bfloat16
    )
    spread = jnp.dot(coupling, selector, preferred_element_type=jnp.float32).astype(jnp.bfloat16)
    front_index = jnp.arange(front, dtype=jnp.int32)[:, None]
    leaf_half = jnp.dot(inverse, leaf_rhs[0], preferred_element_type=jnp.float32).astype(
        jnp.bfloat16
    )
    carried = transposed(spread, leaf_half)
    solved_list = []
    halving_list = []
    for level_index in range(levels):
        columns = carried.shape[1]
        own_bit = position >> level_index & 1
        retained = lax.dynamic_slice_in_dim(carried, own_bit * (columns // 2), columns // 2, 1)
        outgoing = lax.dynamic_slice_in_dim(
            carried, (1 - own_bit) * (columns // 2), columns // 2, 1
        )
        summed = retained + partner_2(outgoing, "leaf", level_index)
        live_rows = front_index < front_sizes[level_index]
        operand = jnp.where(live_rows, summed, 0.0).astype(jnp.bfloat16)
        solved = jnp.where(
            live_rows,
            jnp.dot(front_inverse[0, level_index, 0], operand, preferred_element_type=jnp.float32),
            0.0,
        ).astype(jnp.bfloat16)
        solved_list.append(solved)
        halving_list.append(True)
        if level_index < levels - 1:
            carried = transposed(front_coupling[0, level_index, 0], solved)
    current = solved_list[-1]
    for level_index in range(levels - 2, -1, -1):
        current = widen(current, level_index + 1, position)
        lifted_up = jnp.dot(
            front_coupling[0, level_index, 0], current, preferred_element_type=jnp.float32
        ).astype(jnp.bfloat16)
        correction = jnp.dot(
            front_inverse[0, level_index, 0], lifted_up, preferred_element_type=jnp.float32
        )
        live_rows = front_index < front_sizes[level_index]
        current = jnp.where(
            live_rows, solved_list[level_index].astype(jnp.float32) - correction, 0.0
        ).astype(jnp.bfloat16)
    current = widen(current, 0, position)
    lifted = jnp.dot(spread, current, preferred_element_type=jnp.float32).astype(jnp.bfloat16)
    weight = shift_weight[0]
    weighted = weight * (
        leaf_half.astype(jnp.float32) - jnp.dot(inverse, lifted, preferred_element_type=jnp.float32)
    )
    result = lax.psum_scatter(weighted, "shift", scatter_dimension=0, tiled=True)
    return result[None]


def solution(mesh):
    in_specs = (
        P("leaf", None, None),
        P("shift", "leaf", None, None),
        P("shift", "leaf", None, None),
        P("leaf", None),
        P(),
        P("shift", None, "leaf", None, None),
        P("shift", None, "leaf", None, None),
        P("shift"),
    )
    out_specs = P("leaf", "shift", None)
    return jax.shard_map(body, mesh=mesh, in_specs=in_specs, out_specs=out_specs, check_vma=False)
```

profile of v0, /device:TPU:1, one launch (start us, length us, event | category | flops | bytes accessed | tf_op | source)
XLA Modules:
  0.0 196.6 jit_solution(3682693548286623951)
XLA Ops:
  8.1 4.0 %fusion.6 = bf16[1024,1024]{1,0:T(8,128)(2,1)S(1)} fusion(bf16[1,1024,1024]{2,1,0:T(8,128)(2,1)} %param.8, bf16[1,1,1024,1024]{3,2,1,0:T(8,128)(2,1)S(1)} %copy-done), kind=kOutput, calls=%fused_computation.7 | convolution fusion | flops 2148532224 | bytes 6291456 | tf_op jit(solution)/shard_map/dot_general | solution.py:47
  13.3 1.8 fusion.191
  15.2 1.7 copy-done.1
  20.9 2.1 %collective-permute-done = f32[768,512]{1,0:T(8,128)} collective-permute-done((f32[768,512]{1,0:T(8,128)}, f32[768,512]{1,0:T(8,128)}, u32[]{:S(2)}, u32[]{:S(2)}) %collective-permute-start) | collective-permute-done | bytes 1572896 | tf_op jit(solution)/shard_map/ppermute | solution.py:10
  23.0 3.2 %select_convert_fusion.1 = bf16[512,768]{1,0:T(8,128)(2,1)S(1)} fusion(bf16[1,5,1,768,768]{4,3,2,1,0:T(8,128)(2,1)} %param.13, f32[768,512]{1,0:T(8,128)} %collective-permute-done, f32[768,1024]{1,0:T(8,128)} %copy-done.1, s32[]{:T(128)S(6)} %select_n.143, pred[768]{0:T(1024)(128)(4,1)S(1)} %iota_compare_fusion.5), kind=kOutput, calls=%fused_computation.14 | convolution fusion | flops 605945856 | bytes 5113860 | tf_op jit(solution)/shard_map/dot_general | solution.py:65
  26.2 2.3 %fusion.44 = f32[512,768]{1,0:T(8,128)S(1)} fusion(bf16[512,768]{1,0:T(8,128)(2,1)S(1)} %select_convert_fusion.1, bf16[1,4,1,768,768]{4,3,2,1,0:T(8,128)(2,1)} %param.14), kind=kOutput, calls=%fused_computation.50 | convolution fusion | flops 603979776 | bytes 3538944 | tf_op jit(solution)/shard_map/dot_general | solution.py:14
  31.9 16.8 %collective-permute-done.1 = f32[768,256]{0,1:T(8,128)} collective-permute-done((f32[768,256]{0,1:T(8,128)S(1)}, f32[768,256]{0,1:T(8,128)}, u32[]{:S(2)}, u32[]{:S(2)}) %collective-permute-start.1) | collective-permute-done | bytes 786464 | tf_op jit(solution)/shard_map/ppermute | solution.py:10
  48.7 2.3 %fusion.17 = bf16[256,768]{1,0:T(8,128)(2,1)S(1)} fusion(bf16[1,5,1,768,768]{4,3,2,1,0:T(8,128)(2,1)} %param.13, f32[768,256]{0,1:T(8,128)} %collective-permute-done.1, f32[512,768]{1,0:T(8,128)} %copy-done.2, s32[]{:T(128)S(6)} %select_n.148, pred[768]{0:T(1024)(128)(4,1)S(1)} %iota_compare_fusion.4), kind=kOutput, calls=%fused_computation.21 | convolution fusion | flops 302972928 | bytes 3147780 | tf_op jit(solution)/shard_map/dot_general | solution.py:65
  51.0 1.7 fusion.39
  53.5 3.0 %collective-permute-start.2 = (f32[768,128]{0,1:T(8,128)}, f32[768,128]{0,1:T(8,128)}, u32[]{:S(2)}, u32[]{:S(2)}) collective-permute-start(f32[768,128]{0,1:T(8,128)} %dynamic-slice_bitcast_fusion.1), channel_id=1, source_target_pairs={{0,4},{1,5},{2,6},{3,7},{4,0},{5,1},{6,2},{7,3},{8,12},{9,13},{10,... | collective-permute-start | bytes 1179656 | tf_op jit(solution)/shard_map/ppermute | solution.py:10
  57.2 7.7 %collective-permute-done.2 = f32[768,128]{0,1:T(8,128)} collective-permute-done((f32[768,128]{0,1:T(8,128)}, f32[768,128]{0,1:T(8,128)}, u32[]{:S(2)}, u32[]{:S(2)}) %collective-permute-start.2) | collective-permute-done | bytes 393248 | tf_op jit(solution)/shard_map/ppermute | solution.py:10
  64.9 1.9 fusion.50
  66.8 1.6 fusion.33
  70.4 2.7 %collective-permute-done.3 = f32[768,64]{0,1:T(8,128)S(1)} collective-permute-done((f32[768,64]{0,1:T(8,128)S(1)}, f32[768,64]{0,1:T(8,128)S(1)}, u32[]{:S(2)}, u32[]{:S(2)}) %collective-permute-start.3) | collective-permute-done | bytes 196640 | tf_op jit(solution)/shard_map/ppermute | solution.py:10
  73.1 1.8 fusion.79
  74.8 1.6 fusion.25
  76.5 2.8 %collective-permute-start.4 = (f32[768,32]{0,1:T(8,128)S(1)}, f32[768,32]{0,1:T(8,128)S(1)}, u32[]{:S(2)}, u32[]{:S(2)}) collective-permute-start(f32[768,32]{0,1:T(8,128)S(1)} %dynamic-slice_bitcast_fusion.3), channel_id=1, source_target_pairs={{0,16},{1,17},{2,18},{3,19},{4,20},{5,21},{6,22},{7,23},{8,24},{9,... | collective-permute-start | bytes 294920 | tf_op jit(solution)/shard_map/ppermute | solution.py:10
  81.5 1.7 fusion.93
  83.2 2.8 %collective-permute-start.5 = (bf16[768,32]{0,1:T(8,128)(2,1)S(1)}, bf16[768,32]{0,1:T(8,128)(2,1)S(1)}, u32[]{:S(2)}, u32[]{:S(2)}) collective-permute-start(bf16[768,32]{0,1:T(8,128)(2,1)S(1)} %fusion.93), channel_id=1, source_target_pairs={{0,16},{1,17},{2,18},{3,19},{4,20},{5,21},{6,22},{7,23},{8,24},{9,... | collective-permute-start | bytes 147464 | tf_op jit(solution)/shard_map/ppermute | solution.py:10
  86.0 1.7 collective-permute-done.5
  87.7 2.5 %fusion.82 = bf16[768,64]{0,1:T(8,128)(2,1)S(1)} fusion(bf16[1,4,1,768,768]{4,3,2,1,0:T(8,128)(2,1)} %param.14, bf16[1,5,1,768,768]{4,3,2,1,0:T(8,128)(2,1)} %param.13, bf16[64,768]{1,0:T(8,128)(2,1)S(1)} %fusion.79, bf16[768,32]{0,1:T(8,128)(2,1)S(1)} %get-tuple-element.14, bf16[768,32]{0,1:T(8,128)(2,1)S(1)} %get-tuple-element.13, ...), kind=kOutput, calls=%fused_computation.67 | convolution fusion | flops 151437312 | bytes 2654976 | tf_op jit(solution)/shard_map/dot_general | solution.py:78
  91.6 2.2 %collective-permute-done.6 = bf16[768,64]{0,1:T(8,128)(2,1)S(1)} collective-permute-done((bf16[768,64]{0,1:T(8,128)(2,1)S(1)}, bf16[768,64]{0,1:T(8,128)(2,1)S(1)}, u32[]{:S(2)}, u32[]{:S(2)}) %collective-permute-start.6) | collective-permute-done | bytes 98336 | tf_op jit(solution)/shard_map/ppermute | solution.py:10
  93.9 2.6 %fusion.59 = bf16[768,128]{0,1:T(8,128)(2,1)S(1)} fusion(bf16[1,4,1,768,768]{4,3,2,1,0:T(8,128)(2,1)} %param.14, bf16[1,5,1,768,768]{4,3,2,1,0:T(8,128)(2,1)} %param.13, bf16[128,768]{1,0:T(8,128)(2,1)S(1)} %fusion.50, bf16[768,64]{0,1:T(8,128)(2,1)S(1)} %get-tuple-element.12, bf16[768,64]{0,1:T(8,128)(2,1)S(1)} %get-tuple-element.11, ...), kind=kOutput, calls=%fused_computation.60 | convolution fusion | flops 302874624 | bytes 2949888 | tf_op jit(solution)/shard_map/dot_general | solution.py:78
  96.4 3.2 %collective-permute-start.7 = (bf16[768,128]{0,1:T(8,128)(2,1)S(1)}, bf16[768,128]{0,1:T(8,128)(2,1)S(1)}, u32[]{:S(2)}, u32[]{:S(2)}) collective-permute-start(bf16[768,128]{0,1:T(8,128)(2,1)S(1)} %fusion.59), channel_id=1, source_target_pairs={{0,4},{1,5},{2,6},{3,7},{4,0},{5,1},{6,2},{7,3},{8,12},{9,13},{10,... | collective-permute-start | bytes 589832 | tf_op jit(solution)/shard_map/ppermute | solution.py:10
  99.6 3.1 %collective-permute-done.7 = bf16[768,128]{0,1:T(8,128)(2,1)S(1)} collective-permute-done((bf16[768,128]{0,1:T(8,128)(2,1)S(1)}, bf16[768,128]{0,1:T(8,128)(2,1)S(1)}, u32[]{:S(2)}, u32[]{:S(2)}) %collective-permute-start.7) | collective-permute-done | bytes 196640 | tf_op jit(solution)/shard_map/ppermute | solution.py:10
  102.7 2.6 %fusion.19 = bf16[768,256]{0,1:T(8,128)(2,1)S(1)} fusion(bf16[1,4,1,768,768]{4,3,2,1,0:T(8,128)(2,1)} %param.14, bf16[1,5,1,768,768]{4,3,2,1,0:T(8,128)(2,1)} %param.13, bf16[256,768]{1,0:T(8,128)(2,1)S(1)} %fusion.17, bf16[768,128]{0,1:T(8,128)(2,1)S(1)} %get-tuple-element.10, bf16[768,128]{0,1:T(8,128)(2,1)S(1)} %get-tuple-element.9, ...), kind=kOutput, calls=%fused_computation.25 | convolution fusion | flops 605749248 | bytes 3539712 | tf_op jit(solution)/shard_map/dot_general | solution.py:78
  106.7 7.4 %collective-permute-done.8 = bf16[768,256]{0,1:T(8,128)(2,1)S(1)} collective-permute-done((bf16[768,256]{0,1:T(8,128)(2,1)S(1)}, bf16[768,256]{0,1:T(8,128)(2,1)S(1)}, u32[]{:S(2)}, u32[]{:S(2)}) %collective-permute-start.8) | collective-permute-done | bytes 393248 | tf_op jit(solution)/shard_map/ppermute | solution.py:10
  114.9 3.5 %fusion.15 = bf16[768,512]{0,1:T(8,128)(2,1)S(1)} fusion(bf16[512,768]{1,0:T(8,128)(2,1)} %copy-done.5, bf16[1,5,1,768,768]{4,3,2,1,0:T(8,128)(2,1)} %param.13, bf16[1,4,1,768,768]{4,3,2,1,0:T(8,128)(2,1)} %param.14, bf16[768,256]{0,1:T(8,128)(2,1)} %get-tuple-element.8, bf16[768,256]{0,1:T(8,128)(2,1)S(1)} %get-tuple-element.7, ...), kind=kOutput, calls=%fused_computation.17 | convolution fusion | flops 1211498496 | bytes 4719360 | tf_op jit(solution)/shard_map/dot_general | solution.py:78
  118.4 8.3 %collective-permute-start.9 = (bf16[768,512]{0,1:T(8,128)(2,1)S(1)}, bf16[768,512]{0,1:T(8,128)(2,1)}, u32[]{:S(2)}, u32[]{:S(2)}) collective-permute-start(bf16[768,512]{0,1:T(8,128)(2,1)S(1)} %fusion.15), channel_id=1, source_target_pairs={{0,1},{1,0},{2,3},{3,2},{4,5},{5,4},{6,7},{7,6},{8,9},{9,8},{10,11... | collective-permute-start | bytes 2359304 | tf_op jit(solution)/shard_map/ppermute | solution.py:10
  128.7 2.4 %broadcast_select_fusion.1 = (bf16[768,512]{0,1:T(8,128)(2,1)}, bf16[768,512]{0,1:T(8,128)(2,1)}) fusion(bf16[768,512]{0,1:T(8,128)(2,1)S(1)} %fusion.15, bf16[768,512]{0,1:T(8,128)(2,1)} %collective-permute-done.9, pred[]{:T(512)S(6)} %eq.39), kind=kLoop, calls=%fused_computation.98 | loop fusion | flops 786432 | bytes 3145729 | tf_op jit(solution)/shard_map/jit(_where)/select_n | solution.py:22
  131.1 8.6 %fusion = f32[1024,1024]{1,0:T(8,128)} fusion(bf16[1024,1024]{1,0:T(8,128)(2,1)} %copy-done.7, bf16[1,1,1024,1024]{3,2,1,0:T(8,128)(2,1)S(1)} %copy-done, f32[]{:T(128)} %bitcast.157, bf16[768,1024]{1,0:T(8,128)(2,1)} %copy-done.6, bf16[768,512]{0,1:T(8,128)(2,1)} %get-tuple-element.6, bf16[768,512]{0,1:T(8,128)(2,1)} %get-tuple-element.5), kind=kOutput, calls=%fused_computation.1 | convolution fusion | flops 3765436416 | bytes 11534340 | tf_op jit(solution)/shard_map/dot_general | solution.py:89
  139.7 50.0 %reduce-scatter.2.cloned.1.call-done = f32[256,1024]{1,0:T(8,128)} async-done(((f32[1024,1024]{1,0:T(8,128)}), f32[256,1024]{1,0:T(8,128)}) %reduce-scatter.2.cloned.1.call-update) | async-done | bytes 1048592 | tf_op jit(solution)/shard_map/reduce_scatter | solution.py:91
  (41 shorter events, 20.7 us)
Async XLA Ops:
  6.5 1.6 copy-start
  6.5 183.2 %reduce-scatter.2.cloned.1.call-start = ((), (), s32[]{:S(2)}) async-start(), calls=%async_computation.1 | async-start | bytes 5242880 | tf_op jit(solution)/shard_map/reduce_scatter | solution.py:91
  8.1 4.0 %copy-start.4 = (bf16[1,1,1024,384]{3,2,1,0:T(8,128)(2,1)S(1)}, bf16[1,1,1024,384]{3,2,1,0:T(8,128)(2,1)}, u32[]{:S(2)}) copy-start(bf16[1,1,1024,384]{3,2,1,0:T(8,128)(2,1)} %param.10) | copy-start | bytes 2359300
  12.2 3.0 %copy-start.7 = (bf16[1024,1024]{1,0:T(8,128)(2,1)}, bf16[1024,1024]{1,0:T(8,128)(2,1)S(1)}, u32[]{:S(2)}) copy-start(bf16[1024,1024]{1,0:T(8,128)(2,1)S(1)} %fusion.6) | copy-start | bytes 6291460
  13.3 1.8 copy-start.6
  15.2 1.7 copy-start.1
  16.9 2.7 %copy-start.3 = (s32[5]{0:T(128)S(1)}, s32[5]{0:T(128)}, u32[]{:S(2)}) copy-start(s32[5]{0:T(128)} %param.12) | copy-start | bytes 64
  18.2 4.8 %collective-permute-start = (f32[768,512]{1,0:T(8,128)}, f32[768,512]{1,0:T(8,128)}, u32[]{:S(2)}, u32[]{:S(2)}) collective-permute-start(f32[768,512]{1,0:T(8,128)} %constant_dynamic-slice_fusion), channel_id=1, source_target_pairs={{0,1},{1,0},{2,3},{3,2},{4,5},{5,4},{6,7},{7,6},{8,9},{9,8},{10,11... | collective-permute-start | bytes 4718600 | tf_op jit(solution)/shard_map/ppermute | solution.py:10
  26.2 3.6 %copy-start.5 = (bf16[512,768]{1,0:T(8,128)(2,1)}, bf16[512,768]{1,0:T(8,128)(2,1)S(1)}, u32[]{:S(2)}) copy-start(bf16[512,768]{1,0:T(8,128)(2,1)S(1)} %select_convert_fusion.1) | copy-start | bytes 2359300
  28.6 1.2 copy-start.2
  29.8 18.9 %collective-permute-start.1 = (f32[768,256]{0,1:T(8,128)S(1)}, f32[768,256]{0,1:T(8,128)}, u32[]{:S(2)}, u32[]{:S(2)}) collective-permute-start(f32[768,256]{0,1:T(8,128)S(1)} %dynamic-slice_bitcast_fusion), channel_id=1, source_target_pairs={{0,2},{1,3},{2,0},{3,1},{4,6},{5,7},{6,4},{7,5},{8,10},{9,11},{10,... | collective-permute-start | bytes 2359304 | tf_op jit(solution)/shard_map/ppermute | solution.py:10
  53.5 11.4 %collective-permute-start.2 = (f32[768,128]{0,1:T(8,128)}, f32[768,128]{0,1:T(8,128)}, u32[]{:S(2)}, u32[]{:S(2)}) collective-permute-start(f32[768,128]{0,1:T(8,128)} %dynamic-slice_bitcast_fusion.1), channel_id=1, source_target_pairs={{0,4},{1,5},{2,6},{3,7},{4,0},{5,1},{6,2},{7,3},{8,12},{9,13},{10,... | collective-permute-start | bytes 1179656 | tf_op jit(solution)/shard_map/ppermute | solution.py:10
  68.5 4.6 %collective-permute-start.3 = (f32[768,64]{0,1:T(8,128)S(1)}, f32[768,64]{0,1:T(8,128)S(1)}, u32[]{:S(2)}, u32[]{:S(2)}) collective-permute-start(f32[768,64]{0,1:T(8,128)S(1)} %dynamic-slice_bitcast_fusion.2), channel_id=1, source_target_pairs={{0,8},{1,9},{2,10},{3,11},{4,12},{5,13},{6,14},{7,15},{8,0},{9,1},... | collective-permute-start | bytes 589832 | tf_op jit(solution)/shard_map/ppermute | solution.py:10
  76.5 5.1 %collective-permute-start.4 = (f32[768,32]{0,1:T(8,128)S(1)}, f32[768,32]{0,1:T(8,128)S(1)}, u32[]{:S(2)}, u32[]{:S(2)}) collective-permute-start(f32[768,32]{0,1:T(8,128)S(1)} %dynamic-slice_bitcast_fusion.3), channel_id=1, source_target_pairs={{0,16},{1,17},{2,18},{3,19},{4,20},{5,21},{6,22},{7,23},{8,24},{9,... | collective-permute-start | bytes 294920 | tf_op jit(solution)/shard_map/ppermute | solution.py:10
  83.2 4.5 %collective-permute-start.5 = (bf16[768,32]{0,1:T(8,128)(2,1)S(1)}, bf16[768,32]{0,1:T(8,128)(2,1)S(1)}, u32[]{:S(2)}, u32[]{:S(2)}) collective-permute-start(bf16[768,32]{0,1:T(8,128)(2,1)S(1)} %fusion.93), channel_id=1, source_target_pairs={{0,16},{1,17},{2,18},{3,19},{4,20},{5,21},{6,22},{7,23},{8,24},{9,... | collective-permute-start | bytes 147464 | tf_op jit(solution)/shard_map/ppermute | solution.py:10
  90.3 3.5 %collective-permute-start.6 = (bf16[768,64]{0,1:T(8,128)(2,1)S(1)}, bf16[768,64]{0,1:T(8,128)(2,1)S(1)}, u32[]{:S(2)}, u32[]{:S(2)}) collective-permute-start(bf16[768,64]{0,1:T(8,128)(2,1)S(1)} %fusion.82), channel_id=1, source_target_pairs={{0,8},{1,9},{2,10},{3,11},{4,12},{5,13},{6,14},{7,15},{8,0},{9,1},... | collective-permute-start | bytes 294920 | tf_op jit(solution)/shard_map/ppermute | solution.py:10
  96.4 6.3 %collective-permute-start.7 = (bf16[768,128]{0,1:T(8,128)(2,1)S(1)}, bf16[768,128]{0,1:T(8,128)(2,1)S(1)}, u32[]{:S(2)}, u32[]{:S(2)}) collective-permute-start(bf16[768,128]{0,1:T(8,128)(2,1)S(1)} %fusion.59), channel_id=1, source_target_pairs={{0,4},{1,5},{2,6},{3,7},{4,0},{5,1},{6,2},{7,3},{8,12},{9,13},{10,... | collective-permute-start | bytes 589832 | tf_op jit(solution)/shard_map/ppermute | solution.py:10
  105.3 8.8 %collective-permute-start.8 = (bf16[768,256]{0,1:T(8,128)(2,1)S(1)}, bf16[768,256]{0,1:T(8,128)(2,1)S(1)}, u32[]{:S(2)}, u32[]{:S(2)}) collective-permute-start(bf16[768,256]{0,1:T(8,128)(2,1)S(1)} %fusion.19), channel_id=1, source_target_pairs={{0,2},{1,3},{2,0},{3,1},{4,6},{5,7},{6,4},{7,5},{8,10},{9,11},{10,... | collective-permute-start | bytes 1179656 | tf_op jit(solution)/shard_map/ppermute | solution.py:10
  118.4 10.3 %collective-permute-start.9 = (bf16[768,512]{0,1:T(8,128)(2,1)S(1)}, bf16[768,512]{0,1:T(8,128)(2,1)}, u32[]{:S(2)}, u32[]{:S(2)}) collective-permute-start(bf16[768,512]{0,1:T(8,128)(2,1)S(1)} %fusion.15), channel_id=1, source_target_pairs={{0,1},{1,0},{2,3},{3,2},{4,5},{5,4},{6,7},{7,6},{8,9},{9,8},{10,11... | collective-permute-start | bytes 2359304 | tf_op jit(solution)/shard_map/ppermute | solution.py:10
Sparse Core Ops, SparseCore 0:
  139.9 49.8 reduce-scatter.1
where the time goes:
time: 197 us
  waiting for transfers between devices  96.7 us (49%)
  matrix products  44.9 us (23%)
  starting transfers between devices  26.9 us (14%)
  between operations  14.3 us (7%)
  other arithmetic  7.32 us (4%)
  local copies, waits for them, and re-layouts  6.48 us (3%)
    reduce_scatter x1, waiting for transfers between devices, body(): lax.psum_scatter(weighted, 'shift', scatter_dimension=0, tiled=True)  50 us
    ppermute x10, waiting for transfers between devices, partner_2(): return lax.ppermute(value, axis, pairs)  46.6 us
    ppermute x10, starting transfers between devices, partner_2(): return lax.ppermute(value, axis, pairs)  26.9 us
    dot_general x4, matrix products, body(): jnp.dot(front_inverse[0, level_index, 0], lifted_up, preferred_element_ty...  11.2 us
    dot_general x5, matrix products, body(): jnp.dot(front_inverse[0, level_index, 0], operand, preferred_element_type...  10.9 us
    dot_general x5, matrix products, transposed(): lax.dot_general(left_matrix, right_matrix, (((0,), (0,)), ((), ())), pref...  9.1 us
    dot_general x1, matrix products, body(): jnp.dot(inverse, lifted, preferred_element_type=jnp.float32)  8.58 us
    dot_general x1, matrix products, body(): jnp.dot(inverse, leaf_rhs[0], preferred_element_type=jnp.float32)  3.99 us
  transfers between devices with their start and end apart: 11, of which 11 were waited for; matrix products, arithmetic and copies ran while one was open for 2% of the time, Pallas kernels for 0%

commit v1 on v0

v1 whole, which is shorter than its diff:
```python
import jax
import jax.numpy as jnp
from jax import lax
from jax.experimental import pallas as pl
from jax.experimental.pallas import tpu as pltpu
from jax.sharding import PartitionSpec as P

F32 = jnp.float32
BF16 = jnp.bfloat16
NN = (((1,), (0,)), ((), ()))
NT = (((1,), (1,)), ((), ()))
TN = (((0,), (0,)), ((), ()))
STREAMS = 2


def mm(left, right, dims):
    return lax.dot_general(left, right, dims, preferred_element_type=F32)


def kernel(
    rhs_hbm,
    ainv_hbm,
    cpl_hbm,
    rows_ref,
    sizes_ref,
    finv_hbm,
    fcpl_hbm,
    weight_ref,
    out_ref,
    rhs,
    ainv,
    cpl,
    finv,
    fcpl,
    select_t,
    reduced,
    half,
    lift,
    pick_op,
    own0,
    send0,
    recv0,
    solved1,
    solved1_other,
    base,
    own1,
    send1,
    recv1,
    solved2,
    own2,
    send2,
    recv2,
    solved3,
    own3,
    send3,
    recv3,
    solved4,
    own4,
    send4,
    recv4,
    back3,
    back3_other,
    back2,
    back2_other,
    zown,
    zsend1,
    zrecv1,
    zsend2,
    zrecv2,
    load_sem,
    send_sem,
    recv_sem,
):
    leaf_order, _ = ainv.shape
    front = finv.shape[-1]
    bound = cpl.shape[-1]
    wide = rhs.shape[-1] // (4 * STREAMS)
    w = wide // 2
    zrows = out_ref.shape[1]

    p = lax.axis_index("leaf")
    z = lax.axis_index("shift")
    nz = 4
    c = lax.rem(p, 2)
    y = lax.rem(p // 2, 4)
    x = p // 8
    h2 = y // 2
    h1 = lax.rem(lax.rem(y, 2) + h2, 2)

    def leaf_of(xx, yy, cc):
        return {"leaf": (xx * 4 + yy) * 2 + cc}

    core_id = leaf_of(x, y, 1 - c)
    y1_id = leaf_of(x, y + 1 - 2 * lax.rem(y, 2), c)
    y3_id = leaf_of(x, 3 - y, c)
    x1_id = leaf_of(x + 1 - 2 * lax.rem(x, 2), y, c)
    x3_id = leaf_of(3 - x, y, c)
    zp_id = {"shift": lax.rem(z + 1, nz)}
    zm_id = {"shift": lax.rem(z + nz - 1, nz)}
    halves = ((1 - h1, 1 - h2), (1 - h1, h2), (h1, 1 - h2), (h1, h2))

    def column(s, q):
        a, b = halves[q]
        return pl.multiple_of(((a * 2 + b) * STREAMS + s) * wide, wide)

    loads = {}

    def load(name, src, dst):
        copy = pltpu.make_async_copy(src, dst, load_sem.at[len(loads)])
        loads[name] = copy
        copy.start()

    load("cpl", cpl_hbm.at[0, 0], cpl)
    load("ainv", ainv_hbm.at[0, 0], ainv)
    for s in range(STREAMS):
        for q in range(4):
            load(
                ("rhs", s, q),
                rhs_hbm.at[0, :, pl.ds(column(s, q), wide)],
                rhs.at[:, pl.ds((s * 4 + q) * wide, wide)],
            )
    for level in range(5):
        load(("finv", level), finv_hbm.at[0, level, 0], finv.at[level])
        if level < 4:
            load(("fcpl", level), fcpl_hbm.at[0, level, 0], fcpl.at[level])

    barrier = pltpu.get_barrier_semaphore()
    partners = (core_id, y1_id, y3_id, x1_id, x3_id, zp_id, zm_id)
    for partner in partners:
        pl.semaphore_signal(
            barrier, inc=1, device_id=partner, device_id_type=pl.DeviceIdType.MESH
        )
    pl.semaphore_wait(barrier, len(partners))

    sent = {}

    def send(name, src, dst, device):
        copy = pltpu.make_async_remote_copy(
            src_ref=src,
            dst_ref=dst,
            send_sem=send_sem.at[len(sent)],
            recv_sem=recv_sem.at[len(sent)],
            device_id=device,
            device_id_type=pl.DeviceIdType.MESH,
        )
        sent[name] = copy
        copy.start()

    def live(value, level):
        lane = lax.broadcasted_iota(jnp.int32, value.shape, len(value.shape) - 1)
        return jnp.where(lane < sizes_ref[level], value, 0.0)

    tiles = range(0, front, 256)

    def solve(operand, level, dst):
        for n in tiles:
            got = mm(operand, finv[level, n : n + 256, :], NT)
            lane = n + lax.broadcasted_iota(jnp.int32, got.shape, 1)
            dst[:, n : n + 256] = jnp.where(lane < sizes_ref[level], got, 0.0).astype(BF16)

    def raise_to(solved, level, keep, out):
        for n in tiles:
            got = mm(solved, fcpl[level, :, n : n + 256], NN)
            if keep is not None:
                keep[:, n : n + 256] = got
            if out is not None:
                out[:, n : n + 256] = got.astype(BF16)

    def descend(parent, level, solved, dst):
        lifted = jnp.concatenate(
            [mm(parent, fcpl[level, n : n + 256, :], NT).astype(BF16) for n in tiles], axis=1
        )
        for n in tiles:
            got = solved[:, n : n + 256].astype(F32) - mm(
                lifted, finv[level, n : n + 256, :], NT
            )
            lane = n + lax.broadcasted_iota(jnp.int32, got.shape, 1)
            dst[:, n : n + 256] = jnp.where(lane < sizes_ref[level], got, 0.0).astype(BF16)

    for n in range(0, front, 256):
        row = n + lax.broadcasted_iota(jnp.int32, (256, bound), 0)
        select_t[n : n + 256, :] = jnp.where(row == rows_ref[...], 1.0, 0.0).astype(BF16)

    loads["cpl"].wait()
    loads["ainv"].wait()
    for n in range(0, leaf_order, 256):
        reduced[:, n : n + 256] = mm(cpl[...], ainv[:, n : n + 256], TN).astype(BF16)

    for s in range(STREAMS):
        for q in range(4):
            loads["rhs", s, q].wait()
            start = (s * 4 + q) * wide
            boundary = mm(reduced[...], rhs[:, start : start + wide], NN)
            boundary_t = jnp.transpose(boundary).astype(BF16)
            for n in tiles:
                placed = mm(boundary_t, select_t[n : n + 256, :], NT)
                low, high = placed[:w], placed[w:]
                own0[s, q * w : q * w + w, n : n + 256] = jnp.where(c == 0, low, high)
                send0[s, q * w : q * w + w, n : n + 256] = jnp.where(c == 0, high, low).astype(
                    BF16
                )
            if q % 2:
                pair = pl.ds((q - 1) * w, 2 * w)
                send(("place", s, q // 2), send0.at[s, pair], recv0.at[s, pair], core_id)

    loads["finv", 0].wait()
    loads["fcpl", 0].wait()
    for pair in range(2):
        for s in range(STREAMS):
            sent["place", s, pair].wait_recv()
            at = slice(pair * 2 * w, (pair + 1) * 2 * w)
            gathered = own0[s, at, :] + recv0[s, at, :].astype(F32)
            operand = live(gathered, 0).astype(BF16)
            place = pl.ds(s * 4 * w + pair * 2 * w, 2 * w)
            solve(operand, 0, solved1.at[place])
            level1 = solved1[s * 4 * w + pair * 2 * w : s * 4 * w + (pair + 1) * 2 * w, :]
            if pair == 0:
                raise_to(level1, 0, None, send1.at[s])
                for q in range(2):
                    at = pl.ds(q * w, w)
                    send(("up1", s, q), send1.at[s, at], recv1.at[s, at], y1_id)
            else:
                raise_to(level1, 0, own1.at[s], None)
    send("solved1", solved1, solved1_other, core_id)

    for n in range(0, leaf_order, 256):
        half[:, n : n + 256] = mm(ainv[...], rhs[:, n : n + 256], NN).astype(BF16)

    for level in range(1, 5):
        loads["finv", level].wait()
        if level < 4:
            loads["fcpl", level].wait()

    for s in range(STREAMS):
        for q in range(2):
            sent["up1", s, q].wait_recv()
            at = slice(q * w, q * w + w)
            operand = live(own1[s, at, :] + recv1[s, at, :].astype(F32), 1).astype(BF16)
            solve(operand, 1, solved2.at[s, pl.ds(q * w, w)])
            level2 = solved2[s, at, :]
            if q == 0:
                raise_to(level2, 1, None, send2.at[s])
                send(("up2", s), send2.at[s], recv2.at[s], y3_id)
            else:
                raise_to(level2, 1, own2.at[s], None)

    lift[...] = mm(ainv[...], cpl[...], NN).astype(BF16)

    for s in range(STREAMS):
        sent["up2", s].wait_recv()
        operand = live(own2[s] + recv2[s].astype(F32), 2).astype(BF16)
        solve(operand, 2, solved3.at[s])
        raise_to(solved3[s], 2, own3.at[s], send3.at[s])
        send(("up3", s), send3.at[s], recv3.at[s], x1_id)

    for n in tiles:
        pick_op[:, n : n + 256] = mm(select_t[...], finv[0, :, n : n + 256], TN).astype(BF16)

    sent["solved1"].wait_recv()
    for s in range(STREAMS):
        for q in range(4):
            at = slice((s * 4 + q) * w, (s * 4 + q + 1) * w)
            mine = solved1[at, :]
            other = solved1_other[at, :]
            both = jnp.concatenate(
                [jnp.where(c == 0, mine, other), jnp.where(c == 0, other, mine)], axis=0
            )
            base[s * 4 + q] = mm(both, select_t[...], NN).astype(BF16)

    for s in range(STREAMS):
        sent["up3", s].wait_recv()
        operand = live(own3[s] + recv3[s].astype(F32), 3).astype(BF16)
        solve(operand, 3, solved4.at[s])
        raise_to(solved4[s], 3, own4.at[s], send4.at[s])
        send(("up4", s), send4.at[s], recv4.at[s], x3_id)

    for s in range(STREAMS):
        sent["up4", s].wait_recv()
        operand = live(own4[s] + recv4[s].astype(F32), 4).astype(BF16)
        back5 = jnp.concatenate(
            [mm(operand, finv[4, n : n + 256, :], NT) for n in tiles], axis=1
        )
        back5 = live(back5, 4).astype(BF16)
        back4 = own4.at[s]
        lifted = jnp.concatenate(
            [mm(back5, fcpl[3, n : n + 256, :], NT).astype(BF16) for n in tiles], axis=1
        )
        back4 = jnp.concatenate(
            [
                solved4[s, :, n : n + 256].astype(F32) - mm(lifted, finv[3, n : n + 256, :], NT)
                for n in tiles
            ],
            axis=1,
        )
        back4 = live(back4, 3).astype(BF16)
        descend(back4, 2, solved3.at[s], back3.at[s])
        send(("down2", s), back3.at[s], back3_other.at[s], y3_id)
        descend(back3[s], 1, solved2.at[s, pl.ds(w, w)], back2.at[s, 3])
        send(("down1", s, 1), back2.at[s, 3], back2.at[s, 1], y1_id)
        send(("core", s, 3), back2.at[s, 3], back2_other.at[s, 3], core_id)

    def contribution(s, q):
        mine = back2[s, q]
        other = back2_other[s, q]
        both = jnp.concatenate(
            [jnp.where(c == 0, mine, other), jnp.where(c == 0, other, mine)], axis=0
        )
        lifted = jnp.concatenate(
            [mm(both, fcpl[0, n : n + 256, :], NT).astype(BF16) for n in tiles], axis=1
        )
        lane_live = lax.broadcasted_iota(jnp.int32, (1, bound), 1)
        picked = base[s * 4 + q].astype(F32) - mm(lifted, pick_op[...], NT) * alive[...]
        picked = picked.astype(BF16)

        def rows_of(shift):
            at = pl.multiple_of(lax.rem(z + shift, nz) * zrows, zrows)
            start = (s * 4 + q) * wide
            value = half[pl.ds(at, zrows), start : start + wide].astype(F32) - mm(
                lift[pl.ds(at, zrows), :], picked, NT
            )
            return weight_ref[0] * value

        return rows_of

    alive = jnp.where(rows_ref[...] < sizes_ref[0], 1.0, 0.0)
    hz = zrows // 2

    def scatter_first(k, s, q):
        rows_of = contribution(s, q)
        far = rows_of(2).astype(BF16)
        zsend1[k] = far
        send(("z1p", k), zsend1.at[k, pl.ds(0, hz)], zrecv1.at[k, pl.ds(0, hz)], zp_id)
        send(("z1m", k), zsend1.at[k, pl.ds(hz, hz)], zrecv1.at[k, pl.ds(hz, hz)], zm_id)
        zown[k, 1] = rows_of(1)
        zown[k, 2] = rows_of(3)
        zown[k, 0] = rows_of(0)

    def scatter_second(k):
        sent["z1p", k].wait_recv()
        zsend2[k, 0, :hz] = (zown[k, 1, :hz] + zrecv1[k, :hz].astype(F32)).astype(BF16)
        zsend2[k, 0, hz:] = zown[k, 1, hz:].astype(BF16)
        send(("z2p", k), zsend2.at[k, 0], zrecv2.at[k, 0], zp_id)
        sent["z1m", k].wait_recv()
        zsend2[k, 1, :hz] = zown[k, 2, :hz].astype(BF16)
        zsend2[k, 1, hz:] = (zown[k, 2, hz:] + zrecv1[k, hz:].astype(F32)).astype(BF16)
        send(("z2m", k), zsend2.at[k, 1], zrecv2.at[k, 1], zm_id)

    steps = []
    for q in (3, 2, 1, 0):
        for s in range(STREAMS):
            steps.append((s, q))
    for k, (s, q) in enumerate(steps):
        if q == 2:
            sent["down2", s].wait_recv()
            descend(back3_other[s], 1, solved2.at[s, pl.ds(0, w)], back2.at[s, 2])
            send(("down1", s, 0), back2.at[s, 2], back2.at[s, 0], y1_id)
            send(("core", s, 2), back2.at[s, 2], back2_other.at[s, 2], core_id)
        elif q < 2:
            sent["down1", s, q].wait_recv()
            send(("core", s, q), back2.at[s, q], back2_other.at[s, q], core_id)
        sent["core", s, q].wait_recv()
        scatter_first(k, s, q)
        if k:
            scatter_second(k - 1)
    scatter_second(len(steps) - 1)
    for k, (s, q) in enumerate(steps):
        sent["z2p", k].wait_recv()
        sent["z2m", k].wait_recv()
        out_ref[0, :, pl.ds(column(s, q), wide)] = (
            zown[k, 0] + zrecv2[k, 0].astype(F32) + zrecv2[k, 1].astype(F32)
        )
    for copy in sent.values():
        copy.wait_send()


def body(
    leaf_rhs,
    leaf_inverse,
    leaf_coupling,
    leaf_rows,
    front_sizes,
    front_inverse,
    front_coupling,
    shift_weight,
):
    order = leaf_inverse.shape[-1]
    columns = leaf_rhs.shape[-1]
    front = front_inverse.shape[-1]
    bound = leaf_coupling.shape[-1]
    wide = columns // (4 * STREAMS)
    w = wide // 2
    zrows = order // lax.axis_size("shift")
    pieces = 4 * STREAMS
    vmem = pltpu.VMEM
    hbm = pl.BlockSpec(memory_space=pl.ANY)
    local = pl.BlockSpec(memory_space=pltpu.VMEM)
    scalar = pl.BlockSpec(memory_space=pltpu.SMEM)
    level = lambda kind: vmem((STREAMS, w, front), kind)
    sends = 2 * STREAMS + 1 + 2 * STREAMS + 3 * STREAMS + STREAMS + 2 * STREAMS + 4 * STREAMS
    sends += 4 * pieces
    return pl.pallas_call(
        kernel,
        out_shape=jax.ShapeDtypeStruct((1, zrows, columns), F32),
        in_specs=[hbm, hbm, hbm, local, scalar, hbm, hbm, scalar],
        out_specs=local,
        scratch_shapes=[
            vmem((order, columns), BF16),
            vmem((order, order), BF16),
            vmem((order, bound), BF16),
            vmem((5, front, front), BF16),
            vmem((4, front, front), BF16),
            vmem((front, bound), BF16),
            vmem((bound, order), BF16),
            vmem((order, columns), BF16),
            vmem((order, bound), BF16),
            vmem((bound, front), BF16),
            vmem((STREAMS, 4 * w, front), F32),
            vmem((STREAMS, 4 * w, front), BF16),
            vmem((STREAMS, 4 * w, front), BF16),
            vmem((STREAMS * 4 * w, front), BF16),
            vmem((STREAMS * 4 * w, front), BF16),
            vmem((pieces, wide, bound), BF16),
            vmem((STREAMS, 2 * w, front), F32),
            vmem((STREAMS, 2 * w, front), BF16),
            vmem((STREAMS, 2 * w, front), BF16),
            vmem((STREAMS, 2 * w, front), BF16),
            level(F32),
            level(BF16),
            level(BF16),
            level(BF16),
            level(F32),
            level(BF16),
            level(BF16),
            level(BF16),
            level(F32),
            level(BF16),
            level(BF16),
            level(BF16),
            level(BF16),
            vmem((STREAMS, 4, w, front), BF16),
            vmem((STREAMS, 4, w, front), BF16),
            vmem((pieces, 3, zrows, wide), F32),
            vmem((pieces, zrows, wide), BF16),
            vmem((pieces, zrows, wide), BF16),
            vmem((pieces, 2, zrows, wide), BF16),
            vmem((pieces, 2, zrows, wide), BF16),
            pltpu.SemaphoreType.DMA((2 + pieces + 9,)),
            pltpu.SemaphoreType.DMA((sends,)),
            pltpu.SemaphoreType.DMA((sends,)),
        ],
        compiler_params=pltpu.CompilerParams(
            collective_id=0, has_side_effects=True, vmem_limit_bytes=60 * 2**20
        ),
    )(
        leaf_rhs,
        leaf_inverse,
        leaf_coupling,
        leaf_rows,
        front_sizes,
        front_inverse,
        front_coupling,
        shift_weight,
    )


def solution(mesh):
    in_specs = (
        P("leaf", None, None),
        P("shift", "leaf", None, None),
        P("shift", "leaf", None, None),
        P("leaf", None),
        P(),
        P("shift", None, "leaf", None, None),
        P("shift", None, "leaf", None, None),
        P("shift"),
    )
    out_specs = P("leaf", "shift", None)
    return jax.shard_map(body, mesh=mesh, in_specs=in_specs, out_specs=out_specs, check_vma=False)
```

time: 197 us -> 77.8 us (0.39)
  waiting for transfers between devices: 96.7 us -> 0 us
  Pallas kernels: 0 us -> 74.1 us
  matrix products: 44.9 us -> 0 us
  starting transfers between devices: 26.9 us -> 0 us
  between operations: 14.3 us -> 0.66 us
  other arithmetic: 7.32 us -> 0 us
  local copies, waits for them, and re-layouts: 6.48 us -> 2.31 us
    pallas_call x0 -> x1, Pallas kernels: none -> 74.1 us  [body(): pl.pallas_call(kernel, out_shape=jax.ShapeDtypeStruct((1, zrows, columns)...]
    reduce_scatter x1 -> x0, waiting for transfers between devices: 50 us -> none  [body(): lax.psum_scatter(weighted, 'shift', scatter_dimension=0, tiled=True)]
    ppermute x10 -> x0, waiting for transfers between devices: 46.6 us -> none  [partner_2(): return lax.ppermute(value, axis, pairs)]
    dot_general x17 -> x0, matrix products: 44.9 us -> none  [the longest x4 11.2 us: body(): jnp.dot(front_inverse[0, level_index, 0], lifted_up, preferred_element_ty...]
    ppermute x10 -> x0, starting transfers between devices: 26.9 us -> none  [partner_2(): return lax.ppermute(value, axis, pairs)]
    select_n x5 -> x0, other arithmetic: 3.25 us -> none  [widen(): lower = jnp.where(own_bit == 0, solved, partner)]
    lt x5 -> x0, other arithmetic: 3.23 us -> none  [body(): live_rows = front_index < front_sizes[level_index]]
    dynamic_slice x5 -> x0, local copies, waits for them, and re-layouts: 2.22 us -> none  [body(): lax.dynamic_slice_in_dim(carried, (1 - own_bit) * (columns // 2), columns...]
  transfers between devices with their start and end apart: 11 -> 0, of which waited for: 11 -> 0; matrix products, arithmetic and copies ran while one was open for 2% -> 0% of each run, Pallas kernels for 0% -> 0%
where the time goes in v1:
time: 77.8 us; the launch traced here: 77.1 us
  Pallas kernels  74.1 us (95%)
  local copies, waits for them, and re-layouts  2.31 us (3%)
    pallas_call x1, Pallas kernels, body(): pl.pallas_call(kernel, out_shape=jax.ShapeDtypeStruct((1, zrows, columns)...  74.1 us
    unnamed x1, local copies, waits for them, and re-layouts  2.31 us

profile of v1, /device:TPU:1, one launch (start us, length us, event | category | flops | bytes accessed | tf_op | source)
XLA Modules:
  0.0 77.1 jit_solution(6244945686448537231)
XLA Ops:
  0.7 74.1 %shard_map.82 = f32[1,256,1024]{2,1,0:T(8,128)} custom-call(bf16[1,1024,1024]{2,1,0:T(8,128)(2,1)} %rhs_hbm.1, bf16[1,1,1024,1024]{3,2,1,0:T(8,128)(2,1)} %ainv_hbm.1, bf16[1,1,1024,384]{3,2,1,0:T(8,128)(2,1)} %cpl_hbm.1, s32[1,384]{1,0:T(1,128)} %rows_ref.1, s32[5]{0:T(128)} %sizes_ref.1, bf16[1,5,1,768,768]{4,3,2,1,0:T(8,128)(2,1)} %finv_hbm.1, ...), custom_call_target="tpu_custom_call" | custom-call | tf_op jit(solution)/shard_map/pallas_call | solution.py:401
  74.8 2.3 %copy.11 = f32[1,256,1024]{2,1,0:T(8,128)} copy(f32[1,256,1024]{2,1,0:T(8,128)} %shard_map.82) | data formatting | bytes 2097152

commit v2 on v1

v2 whole, which is shorter than its diff:
```python
import jax
import jax.numpy as jnp
from jax import lax
from jax.experimental import pallas as pl
from jax.experimental.pallas import tpu as pltpu
from jax.sharding import PartitionSpec as P

F32 = jnp.float32
BF16 = jnp.bfloat16
NN = (((1,), (0,)), ((), ()))
NT = (((1,), (1,)), ((), ()))
TN = (((0,), (0,)), ((), ()))
STREAMS = 2


def mm(left, right, dims):
    return lax.dot_general(left, right, dims, preferred_element_type=F32)


def kernel(
    rhs_hbm,
    ainv_hbm,
    cpl_hbm,
    rows_ref,
    sizes_ref,
    finv_hbm,
    fcpl_hbm,
    weight_ref,
    out_ref,
    rhs,
    ainv,
    cpl,
    cpl_t,
    finv,
    fcpl,
    select,
    select_t,
    half,
    lift,
    pick_op,
    placed,
    recv0,
    solved1,
    base,
    own1,
    send1,
    recv1,
    solved2,
    own2,
    send2,
    recv2,
    solved3,
    own3,
    send3,
    recv3,
    solved4,
    own4,
    send4,
    recv4,
    back3,
    back3_other,
    back2,
    zown,
    zsend1,
    zrecv1,
    zsend2,
    zrecv2,
    load_sem,
    send_sem,
    recv_sem,
):
    leaf_order, _ = ainv.shape
    front = finv.shape[-1]
    bound = cpl.shape[-1]
    wide = rhs.shape[-1] // (4 * STREAMS)
    w = wide // 2
    zrows = out_ref.shape[1]
    nz = leaf_order // zrows

    p = lax.axis_index("leaf")
    z = lax.axis_index("shift")
    c = lax.rem(p, 2)
    y = lax.rem(p // 2, 4)
    x = p // 8
    h2 = y // 2
    h1 = lax.rem(lax.rem(y, 2) + h2, 2)

    def leaf_of(xx, yy, cc):
        return {"leaf": (xx * 4 + yy) * 2 + cc}

    core_id = leaf_of(x, y, 1 - c)
    y1_id = leaf_of(x, y + 1 - 2 * lax.rem(y, 2), c)
    y3_id = leaf_of(x, 3 - y, c)
    x1_id = leaf_of(x + 1 - 2 * lax.rem(x, 2), y, c)
    x3_id = leaf_of(3 - x, y, c)
    zp_id = {"shift": lax.rem(z + 1, nz)}
    zm_id = {"shift": lax.rem(z + nz - 1, nz)}
    halves = ((1 - h1, 1 - h2), (1 - h1, h2), (h1, 1 - h2), (h1, h2))

    barrier = pltpu.get_barrier_semaphore()
    partners = (core_id, y1_id, y3_id, x1_id, x3_id, zp_id, zm_id)
    for partner in partners:
        pl.semaphore_signal(
            barrier, inc=1, device_id=partner, device_id_type=pl.DeviceIdType.MESH
        )

    def column(s, q):
        a, b = halves[q]
        return pl.multiple_of(((a * 2 + b) * STREAMS + s) * wide, wide)

    loads = {}

    def load(name, src, dst):
        copy = pltpu.make_async_copy(src, dst, load_sem.at[len(loads)])
        loads[name] = copy
        copy.start()

    def load_rhs(s, pair):
        for q in (2 * pair, 2 * pair + 1):
            load(
                ("rhs", s, q),
                rhs_hbm.at[0, :, pl.ds(column(s, q), wide)],
                rhs.at[:, pl.ds((s * 4 + q) * wide, wide)],
            )

    def load_level(level):
        load(("finv", level), finv_hbm.at[0, level, 0], finv.at[level])
        if level < 4:
            load(("fcpl", level), fcpl_hbm.at[0, level, 0], fcpl.at[level])

    load("cpl", cpl_hbm.at[0, 0], cpl)
    load_rhs(0, 0)
    load("ainv", ainv_hbm.at[0, 0], ainv)
    load_rhs(1, 0)
    load_level(0)

    sent = {}

    def send(name, src, dst, device):
        copy = pltpu.make_async_remote_copy(
            src_ref=src,
            dst_ref=dst,
            send_sem=send_sem.at[len(sent)],
            recv_sem=recv_sem.at[len(sent)],
            device_id=device,
            device_id_type=pl.DeviceIdType.MESH,
        )
        sent[name] = copy
        copy.start()

    def live(value, level):
        lane = lax.broadcasted_iota(jnp.int32, value.shape, len(value.shape) - 1)
        return jnp.where(lane < sizes_ref[level], value, 0.0)

    tiles = range(0, front, 256)

    def solve(operand, level, dst):
        for n in tiles:
            got = mm(operand, finv[level, n : n + 256, :], NT)
            lane = n + lax.broadcasted_iota(jnp.int32, got.shape, 1)
            got = jnp.where(lane < sizes_ref[level], got, 0.0).astype(BF16)
            dst(n, got)

    def into(ref):
        def put(n, got):
            ref[:, n : n + 256] = got

        return put

    def raise_to(solved, level, keep, out):
        for n in tiles:
            got = mm(solved, fcpl[level, :, n : n + 256], NN)
            if keep is not None:
                keep[:, n : n + 256] = got
            if out is not None:
                out[:, n : n + 256] = got.astype(BF16)

    def descend(parent, level, solved, dst):
        lifted = jnp.concatenate(
            [mm(parent, fcpl[level, n : n + 256, :], NT).astype(BF16) for n in tiles], axis=1
        )
        for n in tiles:
            got = solved[:, n : n + 256].astype(F32) - mm(
                lifted, finv[level, n : n + 256, :], NT
            )
            lane = n + lax.broadcasted_iota(jnp.int32, got.shape, 1)
            dst[:, n : n + 256] = jnp.where(lane < sizes_ref[level], got, 0.0).astype(BF16)

    for n in tiles:
        row = n + lax.broadcasted_iota(jnp.int32, (256, bound), 0)
        chosen = jnp.where(row == rows_ref[...], 1.0, 0.0)
        select_t[n : n + 256, :] = chosen.astype(BF16)
        select[:, n : n + 256] = jnp.transpose(chosen).astype(BF16)

    loads["cpl"].wait()
    cpl_t[...] = jnp.transpose(cpl[...])

    def halve(s, pair):
        loads["rhs", s, 2 * pair].wait()
        loads["rhs", s, 2 * pair + 1].wait()
        start = (s * 4 + 2 * pair) * wide
        half[:, start : start + 2 * wide] = mm(
            ainv[...], rhs[:, start : start + 2 * wide], NN
        ).astype(BF16)

    def place(s, pair):
        start = (s * 4 + 2 * pair) * wide
        boundary = mm(cpl_t[...], half[:, start : start + 2 * wide], NN)
        boundary_t = jnp.transpose(boundary).astype(BF16)
        for n in tiles:
            got = mm(boundary_t, select_t[n : n + 256, :], NT).astype(BF16)
            for q in range(2):
                for core in range(2):
                    at = (2 * q + core) * w
                    placed[s, pair, core, q * w : q * w + w, n : n + 256] = got[at : at + w]
        send(("place", s, pair), placed.at[s, pair, 1 - c], recv0.at[s, pair], core_id)

    def first(s, pair):
        sent["place", s, pair].wait_recv()
        gathered = placed[s, pair, c].astype(F32) + recv0[s, pair].astype(F32)
        operand = live(gathered, 0).astype(BF16)
        got = []

        def put(n, value):
            got.append(value)
            for q in range(2):
                solved1[s * 4 + 2 * pair + q, c, :, n : n + 256] = value[q * w : q * w + w]

        solve(operand, 0, put)
        level1 = jnp.concatenate(got, axis=1)
        if pair == 0:
            raise_to(level1, 0, None, send1.at[s])
            for q in range(2):
                at = pl.ds(q * w, w)
                send(("up1", s, q), send1.at[s, at], recv1.at[s, at], y1_id)
        else:
            raise_to(level1, 0, own1.at[s], None)
        for q in range(2):
            piece = solved1.at[s * 4 + 2 * pair + q, c]
            send(("solved1", s, 2 * pair + q), piece, piece, core_id)

    def second(s, q):
        sent["up1", s, q].wait_recv()
        at = slice(q * w, q * w + w)
        operand = live(own1[s, at, :] + recv1[s, at, :].astype(F32), 1).astype(BF16)
        solve(operand, 1, into(solved2.at[s, pl.ds(q * w, w)]))
        level2 = solved2[s, at, :]
        if q == 0:
            raise_to(level2, 1, None, send2.at[s])
            send(("up2", s), send2.at[s], recv2.at[s], y3_id)
        else:
            raise_to(level2, 1, own2.at[s], None)

    def third(s):
        sent["up2", s].wait_recv()
        operand = live(own2[s] + recv2[s].astype(F32), 2).astype(BF16)
        solve(operand, 2, into(solved3.at[s]))
        raise_to(solved3[s], 2, own3.at[s], send3.at[s])
        send(("up3", s), send3.at[s], recv3.at[s], x1_id)

    def fourth(s):
        sent["up3", s].wait_recv()
        operand = live(own3[s] + recv3[s].astype(F32), 3).astype(BF16)
        solve(operand, 3, into(solved4.at[s]))
        raise_to(solved4[s], 3, own4.at[s], send4.at[s])
        send(("up4", s), send4.at[s], recv4.at[s], x3_id)

    def turn(s):
        sent["up4", s].wait_recv()
        operand = live(own4[s] + recv4[s].astype(F32), 4).astype(BF16)
        got = []
        solve(operand, 4, lambda n, value: got.append(value))
        back5 = jnp.concatenate(got, axis=1)
        lifted = jnp.concatenate(
            [mm(back5, fcpl[3, n : n + 256, :], NT).astype(BF16) for n in tiles], axis=1
        )
        back4 = jnp.concatenate(
            [
                solved4[s, :, n : n + 256].astype(F32) - mm(lifted, finv[3, n : n + 256, :], NT)
                for n in tiles
            ],
            axis=1,
        )
        back4 = live(back4, 3).astype(BF16)
        descend(back4, 2, solved3.at[s], back3.at[s])
        send(("down2", s), back3.at[s], back3_other.at[s], y3_id)
        descend(back3[s], 1, solved2.at[s, pl.ds(w, w)], back2.at[s, 3, c])
        spread(s, 3)

    def spread(s, q):
        piece = back2.at[s, q, c]
        if q >= 2:
            send(("down1", s, q - 2), piece, back2.at[s, q - 2, c], y1_id)
        send(("core", s, q), piece, piece, core_id)

    def lower(s):
        sent["down2", s].wait_recv()
        descend(back3_other[s], 1, solved2.at[s, pl.ds(0, w)], back2.at[s, 2, c])
        spread(s, 2)

    hz = zrows // 2

    def scatter_first(k, s, q):
        both = back2[s, q].reshape(wide, front)
        picked = base[s * 4 + q].astype(F32) - mm(both, pick_op[...], NT)
        picked = picked.astype(BF16)
        start = (s * 4 + q) * wide

        def rows_of(shift):
            at = pl.multiple_of(lax.rem(z + shift, nz) * zrows, zrows)
            value = half[pl.ds(at, zrows), start : start + wide].astype(F32) - mm(
                lift[pl.ds(at, zrows), :], picked, NT
            )
            return weight_ref[0] * value

        zsend1[k] = rows_of(2).astype(BF16)
        send(("z1p", k), zsend1.at[k, pl.ds(0, hz)], zrecv1.at[k, pl.ds(0, hz)], zp_id)
        send(("z1m", k), zsend1.at[k, pl.ds(hz, hz)], zrecv1.at[k, pl.ds(hz, hz)], zm_id)
        zown[k, 1] = rows_of(1)
        zown[k, 2] = rows_of(3)
        zown[k, 0] = rows_of(0)

    def scatter_second(k):
        sent["z1p", k].wait_recv()
        zsend2[k, 0, :hz] = (zown[k, 1, :hz] + zrecv1[k, :hz].astype(F32)).astype(BF16)
        zsend2[k, 0, hz:] = zown[k, 1, hz:].astype(BF16)
        send(("z2p", k), zsend2.at[k, 0], zrecv2.at[k, 0], zp_id)
        sent["z1m", k].wait_recv()
        zsend2[k, 1, :hz] = zown[k, 2, :hz].astype(BF16)
        zsend2[k, 1, hz:] = (zown[k, 2, hz:] + zrecv1[k, hz:].astype(F32)).astype(BF16)
        send(("z2m", k), zsend2.at[k, 1], zrecv2.at[k, 1], zm_id)

    steps = []

    def step(s, q):
        if q < 2:
            sent["down1", s, q].wait_recv()
            send(("core", s, q), back2.at[s, q, c], back2.at[s, q, c], core_id)
        sent["core", s, q].wait_recv()
        k = len(steps)
        steps.append((s, q))
        scatter_first(k, s, q)
        if k:
            scatter_second(k - 1)

    def make_lift():
        lift[...] = mm(ainv[...], cpl[...], NN).astype(BF16)

    def make_pick():
        row = [mm(live(select[...], 0), finv[0, :, n : n + 256], NN).astype(BF16) for n in tiles]
        row = jnp.concatenate(row, axis=1)
        for n in tiles:
            pick_op[:, n : n + 256] = mm(row, fcpl[0, :, n : n + 256], NN).astype(BF16)

    def make_base(s):
        for q in range(4):
            sent["solved1", s, q].wait_recv()
        at = slice(s * 4, s * 4 + 4)
        got = mm(solved1[at].reshape(4 * wide, front), select_t[...], NN).astype(BF16)
        base[at] = got.reshape(4, wide, bound)

    loads["ainv"].wait()
    halve(0, 0)
    load_rhs(0, 1)
    load_rhs(1, 1)
    pl.semaphore_wait(barrier, len(partners))
    place(0, 0)
    for level in range(1, 5):
        load_level(level)
    halve(1, 0)
    loads["finv", 0].wait()
    loads["fcpl", 0].wait()
    first(0, 0)
    place(1, 0)
    halve(0, 1)
    first(1, 0)
    place(0, 1)
    halve(1, 1)
    first(0, 1)
    loads["finv", 1].wait()
    loads["fcpl", 1].wait()
    second(0, 0)
    place(1, 1)
    second(0, 1)
    first(1, 1)
    for level in range(2, 5):
        loads["finv", level].wait()
        if level < 4:
            loads["fcpl", level].wait()
    second(1, 0)
    third(0)
    second(1, 1)
    make_lift()
    third(1)
    make_pick()
    fourth(0)
    make_base(0)
    make_base(1)
    fourth(1)
    turn(0)
    step(0, 3)
    turn(1)
    lower(0)
    step(0, 2)
    step(0, 1)
    step(1, 3)
    lower(1)
    step(0, 0)
    step(1, 2)
    step(1, 1)
    step(1, 0)
    scatter_second(len(steps) - 1)
    for k, (s, q) in enumerate(steps):
        sent["z2p", k].wait_recv()
        sent["z2m", k].wait_recv()
        out_ref[0, :, pl.ds(column(s, q), wide)] = (
            zown[k, 0] + zrecv2[k, 0].astype(F32) + zrecv2[k, 1].astype(F32)
        )
    for copy in sent.values():
        copy.wait_send()


def body(
    leaf_rhs,
    leaf_inverse,
    leaf_coupling,
    leaf_rows,
    front_sizes,
    front_inverse,
    front_coupling,
    shift_weight,
):
    order = leaf_inverse.shape[-1]
    columns = leaf_rhs.shape[-1]
    front = front_inverse.shape[-1]
    bound = leaf_coupling.shape[-1]
    wide = columns // (4 * STREAMS)
    w = wide // 2
    zrows = order // lax.axis_size("shift")
    pieces = 4 * STREAMS
    vmem = pltpu.VMEM
    hbm = pl.BlockSpec(memory_space=pl.ANY)
    local = pl.BlockSpec(memory_space=pltpu.VMEM)
    scalar = pl.BlockSpec(memory_space=pltpu.SMEM)
    level = lambda kind: vmem((STREAMS, w, front), kind)
    sends = 18 * STREAMS + 4 * pieces
    return pl.pallas_call(
        kernel,
        out_shape=jax.ShapeDtypeStruct((1, zrows, columns), F32),
        in_specs=[hbm, hbm, hbm, local, scalar, hbm, hbm, scalar],
        out_specs=local,
        scratch_shapes=[
            vmem((order, columns), BF16),
            vmem((order, order), BF16),
            vmem((order, bound), BF16),
            vmem((bound, order), BF16),
            vmem((5, front, front), BF16),
            vmem((4, front, front), BF16),
            vmem((bound, front), BF16),
            vmem((front, bound), BF16),
            vmem((order, columns), BF16),
            vmem((order, bound), BF16),
            vmem((bound, front), BF16),
            vmem((STREAMS, 2, 2, 2 * w, front), BF16),
            vmem((STREAMS, 2, 2 * w, front), BF16),
            vmem((pieces, 2, w, front), BF16),
            vmem((pieces, wide, bound), BF16),
            vmem((STREAMS, 2 * w, front), F32),
            vmem((STREAMS, 2 * w, front), BF16),
            vmem((STREAMS, 2 * w, front), BF16),
            vmem((STREAMS, 2 * w, front), BF16),
            level(F32),
            level(BF16),
            level(BF16),
            level(BF16),
            level(F32),
            level(BF16),
            level(BF16),
            level(BF16),
            level(F32),
            level(BF16),
            level(BF16),
            level(BF16),
            level(BF16),
            vmem((STREAMS, 4, 2, w, front), BF16),
            vmem((pieces, 3, zrows, wide), F32),
            vmem((pieces, zrows, wide), BF16),
            vmem((pieces, zrows, wide), BF16),
            vmem((pieces, 2, zrows, wide), BF16),
            vmem((pieces, 2, zrows, wide), BF16),
            pltpu.SemaphoreType.DMA((2 + pieces + 9,)),
            pltpu.SemaphoreType.DMA((sends,)),
            pltpu.SemaphoreType.DMA((sends,)),
        ],
        compiler_params=pltpu.CompilerParams(
            collective_id=0, has_side_effects=True, vmem_limit_bytes=60 * 2**20
        ),
    )(
        leaf_rhs,
        leaf_inverse,
        leaf_coupling,
        leaf_rows,
        front_sizes,
        front_inverse,
        front_coupling,
        shift_weight,
    )


def solution(mesh):
    in_specs = (
        P("leaf", None, None),
        P("shift", "leaf", None, None),
        P("shift", "leaf", None, None),
        P("leaf", None),
        P(),
        P("shift", None, "leaf", None, None),
        P("shift", None, "leaf", None, None),
        P("shift"),
    )
    out_specs = P("leaf", "shift", None)
    return jax.shard_map(body, mesh=mesh, in_specs=in_specs, out_specs=out_specs, check_vma=False)
```

time: 77.8 us -> 74.1 us (0.952)
  Pallas kernels: 74.1 us -> 71 us
    pallas_call x1, Pallas kernels: 74.1 us -> 71 us  [body(): pl.pallas_call(kernel, out_shape=jax.ShapeDtypeStruct((1, zrows, columns)...]
where the time goes in v2:
time: 74.1 us; the launch traced here: 73.9 us
  Pallas kernels  71 us (96%)
  local copies, waits for them, and re-layouts  2.31 us (3%)
    pallas_call x1, Pallas kernels, body(): pl.pallas_call(kernel, out_shape=jax.ShapeDtypeStruct((1, zrows, columns)...  71 us
    unnamed x1, local copies, waits for them, and re-layouts  2.31 us

profile of v2, /device:TPU:1, one launch (start us, length us, event | category | flops | bytes accessed | tf_op | source)
XLA Modules:
  0.0 73.9 jit_solution(8295969079799764695)
XLA Ops:
  0.7 71.0 %shard_map.82 = f32[1,256,1024]{2,1,0:T(8,128)} custom-call(bf16[1,1024,1024]{2,1,0:T(8,128)(2,1)} %rhs_hbm.1, bf16[1,1,1024,1024]{3,2,1,0:T(8,128)(2,1)} %ainv_hbm.1, bf16[1,1,1024,384]{3,2,1,0:T(8,128)(2,1)} %cpl_hbm.1, s32[1,384]{1,0:T(1,128)} %rows_ref.1, s32[5]{0:T(128)} %sizes_ref.1, bf16[1,5,1,768,768]{4,3,2,1,0:T(8,128)(2,1)} %finv_hbm.1, ...), custom_call_target="tpu_custom_call" | custom-call | tf_op jit(solution)/shard_map/pallas_call | solution.py:447
  71.6 2.3 %copy.11 = f32[1,256,1024]{2,1,0:T(8,128)} copy(f32[1,256,1024]{2,1,0:T(8,128)} %shard_map.82) | data formatting | bytes 2097152

commit v3 on v2

--- a/solution.py
+++ b/solution.py
@@ -21,12 +21,14 @@
     rhs_hbm,
     ainv_hbm,
     cpl_hbm,
-    rows_ref,
-    sizes_ref,
+    rows_hbm,
+    sizes_hbm,
     finv_hbm,
     fcpl_hbm,
     weight_ref,
     out_ref,
+    rows_ref,
+    sizes_ref,
     rhs,
     ainv,
     cpl,
@@ -128,7 +130,9 @@
         if level < 4:
             load(("fcpl", level), fcpl_hbm.at[0, level, 0], fcpl.at[level])
 
+    load("rows", rows_hbm, rows_ref)
     load("cpl", cpl_hbm.at[0, 0], cpl)
+    load("sizes", sizes_hbm, sizes_ref)
     load_rhs(0, 0)
     load("ainv", ainv_hbm.at[0, 0], ainv)
     load_rhs(1, 0)
@@ -186,6 +190,7 @@
             lane = n + lax.broadcasted_iota(jnp.int32, got.shape, 1)
             dst[:, n : n + 256] = jnp.where(lane < sizes_ref[level], got, 0.0).astype(BF16)
 
+    loads["rows"].wait()
     for n in tiles:
         row = n + lax.broadcasted_iota(jnp.int32, (256, bound), 0)
         chosen = jnp.where(row == rows_ref[...], 1.0, 0.0)
@@ -213,6 +218,8 @@
                 for core in range(2):
                     at = (2 * q + core) * w
                     placed[s, pair, core, q * w : q * w + w, n : n + 256] = got[at : at + w]
+
+    def send_place(s, pair):
         send(("place", s, pair), placed.at[s, pair, 1 - c], recv0.at[s, pair], core_id)
 
     def first(s, pair):
@@ -230,14 +237,16 @@
         level1 = jnp.concatenate(got, axis=1)
         if pair == 0:
             raise_to(level1, 0, None, send1.at[s])
-            for q in range(2):
-                at = pl.ds(q * w, w)
-                send(("up1", s, q), send1.at[s, at], recv1.at[s, at], y1_id)
+            send_up1(s, 0)
         else:
             raise_to(level1, 0, own1.at[s], None)
         for q in range(2):
             piece = solved1.at[s * 4 + 2 * pair + q, c]
             send(("solved1", s, 2 * pair + q), piece, piece, core_id)
+
+    def send_up1(s, q):
+        at = pl.ds(q * w, w)
+        send(("up1", s, q), send1.at[s, at], recv1.at[s, at], y1_id)
 
     def second(s, q):
         sent["up1", s, q].wait_recv()
@@ -340,8 +349,8 @@
         k = len(steps)
         steps.append((s, q))
         scatter_first(k, s, q)
-        if k:
-            scatter_second(k - 1)
+        if k > 1:
+            scatter_second(k - 2)
 
     def make_lift():
         lift[...] = mm(ainv[...], cpl[...], NN).astype(BF16)
@@ -359,56 +368,64 @@
         got = mm(solved1[at].reshape(4 * wide, front), select_t[...], NN).astype(BF16)
         base[at] = got.reshape(4, wide, bound)
 
+    loads["sizes"].wait()
     loads["ainv"].wait()
     halve(0, 0)
     load_rhs(0, 1)
     load_rhs(1, 1)
-    pl.semaphore_wait(barrier, len(partners))
     place(0, 0)
     for level in range(1, 5):
         load_level(level)
     halve(1, 0)
+    place(1, 0)
+    halve(0, 1)
+    pl.semaphore_wait(barrier, len(partners))
+    send_place(0, 0)
+    send_place(1, 0)
     loads["finv", 0].wait()
     loads["fcpl", 0].wait()
+    place(0, 1)
+    send_place(0, 1)
     first(0, 0)
-    place(1, 0)
-    halve(0, 1)
     first(1, 0)
-    place(0, 1)
+    send_up1(0, 1)
+    send_up1(1, 1)
     halve(1, 1)
     first(0, 1)
+    place(1, 1)
+    send_place(1, 1)
     loads["finv", 1].wait()
     loads["fcpl", 1].wait()
     second(0, 0)
-    place(1, 1)
+    first(1, 1)
+    second(1, 0)
     second(0, 1)
-    first(1, 1)
     for level in range(2, 5):
         loads["finv", level].wait()
         if level < 4:
             loads["fcpl", level].wait()
-    second(1, 0)
     third(0)
     second(1, 1)
     make_lift()
     third(1)
     make_pick()
     fourth(0)
+    fourth(1)
+    turn(0)
     make_base(0)
     make_base(1)
-    fourth(1)
-    turn(0)
+    turn(1)
     step(0, 3)
-    turn(1)
     lower(0)
+    step(1, 3)
+    lower(1)
     step(0, 2)
     step(0, 1)
-    step(1, 3)
-    lower(1)
-    step(0, 0)
     step(1, 2)
     step(1, 1)
+    step(0, 0)
     step(1, 0)
+    scatter_second(len(steps) - 2)
     scatter_second(len(steps) - 1)
     for k, (s, q) in enumerate(steps):
         sent["z2p", k].wait_recv()
@@ -439,17 +456,18 @@
     zrows = order // lax.axis_size("shift")
     pieces = 4 * STREAMS
     vmem = pltpu.VMEM
-    hbm = pl.BlockSpec(memory_space=pl.ANY)
+    hbm = pl.BlockSpec(memory_space=pltpu.HBM)
     local = pl.BlockSpec(memory_space=pltpu.VMEM)
-    scalar = pl.BlockSpec(memory_space=pltpu.SMEM)
     level = lambda kind: vmem((STREAMS, w, front), kind)
     sends = 18 * STREAMS + 4 * pieces
     return pl.pallas_call(
         kernel,
         out_shape=jax.ShapeDtypeStruct((1, zrows, columns), F32),
-        in_specs=[hbm, hbm, hbm, local, scalar, hbm, hbm, scalar],
+        in_specs=[hbm] * 7 + [pl.BlockSpec(memory_space=pltpu.SMEM)],
         out_specs=local,
         scratch_shapes=[
+            vmem((1, bound), jnp.int32),
+            pltpu.SMEM((5,), jnp.int32),
             vmem((order, columns), BF16),
             vmem((order, order), BF16),
             vmem((order, bound), BF16),
@@ -488,21 +506,26 @@
             vmem((pieces, zrows, wide), BF16),
             vmem((pieces, 2, zrows, wide), BF16),
             vmem((pieces, 2, zrows, wide), BF16),
-            pltpu.SemaphoreType.DMA((2 + pieces + 9,)),
+            pltpu.SemaphoreType.DMA((4 + pieces + 9,)),
             pltpu.SemaphoreType.DMA((sends,)),
             pltpu.SemaphoreType.DMA((sends,)),
         ],
         compiler_params=pltpu.CompilerParams(
-            collective_id=0, has_side_effects=True, vmem_limit_bytes=60 * 2**20
+            collective_id=0, has_side_effects=True, vmem_limit_bytes=50 * 2**20
         ),
     )(
-        leaf_rhs,
-        leaf_inverse,
-        leaf_coupling,
-        leaf_rows,
-        front_sizes,
-        front_inverse,
-        front_coupling,
+        *(
+            pltpu.with_memory_space_constraint(value, pltpu.HBM)
+            for value in (
+                leaf_rhs,
+                leaf_inverse,
+                leaf_coupling,
+                leaf_rows,
+                front_sizes,
+                front_inverse,
+                front_coupling,
+            )
+        ),
         shift_weight,
     )
 

time: 74.1 us -> 67.9 us (0.916)
  Pallas kernels: 71 us -> 66.2 us
  local copies, waits for them, and re-layouts: 2.31 us -> 0.97 us
    pallas_call x1, Pallas kernels: 71 us -> 66.2 us  [body(): pl.pallas_call(kernel, out_shape=jax.ShapeDtypeStruct((1, zrows, columns)...]
    unnamed x1, local copies, waits for them, and re-layouts: 2.31 us -> 0.97 us
where the time goes in v3:
time: 67.9 us; the launch traced here: 67.8 us
  Pallas kernels  66.2 us (97%)
  local copies, waits for them, and re-layouts  0.97 us (1%)
    pallas_call x1, Pallas kernels, body(): pl.pallas_call(kernel, out_shape=jax.ShapeDtypeStruct((1, zrows, columns)...  66.2 us

profile of v3, /device:TPU:1, one launch (start us, length us, event | category | flops | bytes accessed | tf_op | source)
XLA Modules:
  0.0 67.8 jit_solution(8546313023392753751)
XLA Ops:
  0.7 66.2 %shard_map.82 = f32[1,256,1024]{2,1,0:T(8,128)S(1)} custom-call(bf16[1,1024,1024]{2,1,0:T(8,128)(2,1)} %rhs_hbm.1, bf16[1,1,1024,1024]{3,2,1,0:T(8,128)(2,1)} %ainv_hbm.1, bf16[1,1,1024,384]{3,2,1,0:T(8,128)(2,1)} %cpl_hbm.1, s32[1,384]{1,0:T(1,128)} %rows_hbm.1, s32[5]{0:T(128)} %sizes_hbm.1, bf16[1,5,1,768,768]{4,3,2,1,0:T(8,128)(2,1)} %finv_hbm.1, ...), custom_call_target="tpu_custom_call" | custom-call | tf_op jit(solution)/shard_map/pallas_call | solution.py:463
  66.8 1.0 %copy.11 = f32[1,256,1024]{2,1,0:T(8,128)} copy(f32[1,256,1024]{2,1,0:T(8,128)S(1)} %shard_map.82) | data formatting | bytes 2097152

commit v4 on v3

--- a/solution.py
+++ b/solution.py
@@ -40,6 +40,7 @@
     half,
     lift,
     pick_op,
+    hop,
     placed,
     recv0,
     solved1,
@@ -179,16 +180,20 @@
             if out is not None:
                 out[:, n : n + 256] = got.astype(BF16)
 
+    def make_hop(level):
+        for n in tiles:
+            hop[level - 1, :, n : n + 256] = mm(
+                finv[level], fcpl[level, :, n : n + 256], NN
+            ).astype(BF16)
+
     def descend(parent, level, solved, dst):
-        lifted = jnp.concatenate(
-            [mm(parent, fcpl[level, n : n + 256, :], NT).astype(BF16) for n in tiles], axis=1
-        )
         for n in tiles:
             got = solved[:, n : n + 256].astype(F32) - mm(
-                lifted, finv[level, n : n + 256, :], NT
+                parent, hop[level - 1, n : n + 256, :], NT
             )
             lane = n + lax.broadcasted_iota(jnp.int32, got.shape, 1)
-            dst[:, n : n + 256] = jnp.where(lane < sizes_ref[level], got, 0.0).astype(BF16)
+            got = jnp.where(lane < sizes_ref[level], got, 0.0).astype(BF16)
+            dst(n, got)
 
     loads["rows"].wait()
     for n in tiles:
@@ -280,20 +285,12 @@
         got = []
         solve(operand, 4, lambda n, value: got.append(value))
         back5 = jnp.concatenate(got, axis=1)
-        lifted = jnp.concatenate(
-            [mm(back5, fcpl[3, n : n + 256, :], NT).astype(BF16) for n in tiles], axis=1
-        )
-        back4 = jnp.concatenate(
-            [
-                solved4[s, :, n : n + 256].astype(F32) - mm(lifted, finv[3, n : n + 256, :], NT)
-                for n in tiles
-            ],
-            axis=1,
-        )
-        back4 = live(back4, 3).astype(BF16)
-        descend(back4, 2, solved3.at[s], back3.at[s])
+        got = []
+        descend(back5, 3, solved4.at[s], lambda n, value: got.append(value))
+        back4 = jnp.concatenate(got, axis=1)
+        descend(back4, 2, solved3.at[s], into(back3.at[s]))
         send(("down2", s), back3.at[s], back3_other.at[s], y3_id)
-        descend(back3[s], 1, solved2.at[s, pl.ds(w, w)], back2.at[s, 3, c])
+        descend(back3[s], 1, solved2.at[s, pl.ds(w, w)], into(back2.at[s, 3, c]))
         spread(s, 3)
 
     def spread(s, q):
@@ -304,7 +301,7 @@
 
     def lower(s):
         sent["down2", s].wait_recv()
-        descend(back3_other[s], 1, solved2.at[s, pl.ds(0, w)], back2.at[s, 2, c])
+        descend(back3_other[s], 1, solved2.at[s, pl.ds(0, w)], into(back2.at[s, 2, c]))
         spread(s, 2)
 
     hz = zrows // 2
@@ -341,16 +338,15 @@
 
     steps = []
 
+    def relay(s, q):
+        sent["down1", s, q].wait_recv()
+        send(("core", s, q), back2.at[s, q, c], back2.at[s, q, c], core_id)
+
     def step(s, q):
-        if q < 2:
-            sent["down1", s, q].wait_recv()
-            send(("core", s, q), back2.at[s, q, c], back2.at[s, q, c], core_id)
         sent["core", s, q].wait_recv()
         k = len(steps)
         steps.append((s, q))
         scatter_first(k, s, q)
-        if k > 1:
-            scatter_second(k - 2)
 
     def make_lift():
         lift[...] = mm(ainv[...], cpl[...], NN).astype(BF16)
@@ -378,55 +374,68 @@
         load_level(level)
     halve(1, 0)
     place(1, 0)
-    halve(0, 1)
     pl.semaphore_wait(barrier, len(partners))
     send_place(0, 0)
     send_place(1, 0)
+    halve(0, 1)
     loads["finv", 0].wait()
     loads["fcpl", 0].wait()
+    first(0, 0)
+    send_up1(0, 1)
+    first(1, 0)
+    send_up1(1, 1)
     place(0, 1)
     send_place(0, 1)
-    first(0, 0)
-    first(1, 0)
-    send_up1(0, 1)
-    send_up1(1, 1)
     halve(1, 1)
     first(0, 1)
-    place(1, 1)
-    send_place(1, 1)
     loads["finv", 1].wait()
     loads["fcpl", 1].wait()
     second(0, 0)
-    first(1, 1)
-    second(1, 0)
+    place(1, 1)
+    send_place(1, 1)
     second(0, 1)
     for level in range(2, 5):
         loads["finv", level].wait()
         if level < 4:
             loads["fcpl", level].wait()
+    first(1, 1)
+    second(1, 0)
+    make_hop(1)
+    make_hop(2)
     third(0)
     second(1, 1)
     make_lift()
     third(1)
+    make_hop(3)
+    fourth(0)
     make_pick()
-    fourth(0)
+    make_base(0)
+    make_base(1)
     fourth(1)
     turn(0)
-    make_base(0)
-    make_base(1)
+    step(0, 3)
     turn(1)
-    step(0, 3)
+    scatter_second(0)
     lower(0)
     step(1, 3)
+    relay(0, 1)
+    step(0, 2)
+    scatter_second(1)
     lower(1)
-    step(0, 2)
     step(0, 1)
+    scatter_second(2)
+    relay(0, 0)
+    relay(1, 1)
     step(1, 2)
+    scatter_second(3)
+    step(0, 0)
+    scatter_second(4)
+    relay(1, 0)
     step(1, 1)
-    step(0, 0)
+    scatter_second(5)
     step(1, 0)
-    scatter_second(len(steps) - 2)
-    scatter_second(len(steps) - 1)
+    scatter_second(6)
+    scatter_second(7)
     for k, (s, q) in enumerate(steps):
         sent["z2p", k].wait_recv()
         sent["z2m", k].wait_recv()
@@ -479,6 +488,7 @@
             vmem((order, columns), BF16),
             vmem((order, bound), BF16),
             vmem((bound, front), BF16),
+            vmem((3, front, front), BF16),
             vmem((STREAMS, 2, 2, 2 * w, front), BF16),
             vmem((STREAMS, 2, 2 * w, front), BF16),
             vmem((pieces, 2, w, front), BF16),

time: 67.9 us -> 66.4 us (0.978); the launches traced: 67.8 us -> 65.5 us
  Pallas kernels: 66.2 us -> 63.9 us
    pallas_call x1, Pallas kernels: 66.2 us -> 63.9 us  [body(): pl.pallas_call(kernel, out_shape=jax.ShapeDtypeStruct((1, zrows, columns)...]
where the time goes in v4:
time: 66.4 us; the launch traced here: 65.5 us
  Pallas kernels  63.9 us (96%)
  local copies, waits for them, and re-layouts  0.97 us (1%)
    pallas_call x1, Pallas kernels, body(): pl.pallas_call(kernel, out_shape=jax.ShapeDtypeStruct((1, zrows, columns)...  63.9 us

profile of v4, /device:TPU:1, one launch (start us, length us, event | category | flops | bytes accessed | tf_op | source)
XLA Modules:
  0.0 65.5 jit_solution(12954778655715257049)
XLA Ops:
  0.7 63.9 %shard_map.82 = f32[1,256,1024]{2,1,0:T(8,128)S(1)} custom-call(bf16[1,1024,1024]{2,1,0:T(8,128)(2,1)} %rhs_hbm.1, bf16[1,1,1024,1024]{3,2,1,0:T(8,128)(2,1)} %ainv_hbm.1, bf16[1,1,1024,384]{3,2,1,0:T(8,128)(2,1)} %cpl_hbm.1, s32[1,384]{1,0:T(1,128)} %rows_hbm.1, s32[5]{0:T(128)} %sizes_hbm.1, bf16[1,5,1,768,768]{4,3,2,1,0:T(8,128)(2,1)} %finv_hbm.1, ...), custom_call_target="tpu_custom_call" | custom-call | tf_op jit(solution)/shard_map/pallas_call | solution.py:472
  64.5 1.0 %copy.11 = f32[1,256,1024]{2,1,0:T(8,128)} copy(f32[1,256,1024]{2,1,0:T(8,128)S(1)} %shard_map.82) | data formatting | bytes 2097152
